TPU v7x, 512 devices: a whole 4x8x8 slice. The times are simulated.
512 devices in a mesh: seq: 64 (over y, z), head: 8 (over x, core).
Axes of the slice: x: 4, y: 8, z: 8, core: 2. Of those that a mesh axis runs over, the one named last changes fastest.
Arguments:
- queries: bfloat16 [16384, 2048], P('seq', 'head'), may hold values from -4 to 4
- first_pair_keys: bfloat16 [16384, 1024], P('seq', 'head'), may hold values from -4 to 4
- first_pair_values: bfloat16 [16384, 1024], P('seq', 'head'), may hold values from -6 to 6
- second_pair_keys: bfloat16 [16384, 1024], P('seq', 'head'), may hold values from -4 to 4
- second_pair_values: bfloat16 [16384, 1024], P('seq', 'head'), may hold values from -6 to 6
- out_weight: bfloat16 [2048, 8192], P('seq', 'head'), may hold values from -0.125 to 0.125
Outputs:
- attended: bfloat16 [16384, 2048], P('seq', 'head')
- projected: bfloat16 [16384, 8192], P('seq', 'head')
All inputs are finite; a program needn't handle non-finite values.
Results may differ from a plain program's by a relative error of at most 0.0064.
Values may be sent and summed in bfloat16 or wider, within the bound.
No kernel may reach another device: no remote copies, remote signals or barrier semaphores. Data moves between devices by JAX's collectives and lax.ppermute only.
A program may use at most 64 MiB of HBM per device.

v0:
```python
import math

import jax
import jax.numpy as jnp
from jax import lax
from jax.sharding import PartitionSpec as P

HEAD_SIZE = 128
GROUP_QUERIES = 2
FIRST_WINDOW = 512
SECOND_WINDOW = 32


def passed_along(x, axis, by):
    size = lax.axis_size(axis)
    pairs = [(i, i + by) for i in range(size) if 0 <= i + by < size]
    return lax.ppermute(x, axis, pairs)


def attend_block(query_rows, first_rows, first_vals, second_win, second_vwin, query_pos, key_pos):
    score_scale = HEAD_SIZE ** (-0.5)
    query_mod = (
        query_rows.astype(jnp.float32)[:, None] * second_win.astype(jnp.float32)[:, :, :, None, :]
    ).astype(jnp.bfloat16)
    scores = (
        jnp.einsum("itvgd,jvd->ivgtj", query_mod, first_rows, preferred_element_type=jnp.float32)
        * score_scale
    )
    key_lag = query_pos[:, None] - key_pos[None, :]
    first_ok = (key_lag >= 0) & (key_lag < FIRST_WINDOW) & (key_pos[None, :] >= 0)
    offsets = jnp.arange(SECOND_WINDOW, dtype=jnp.int32)
    second_ok = query_pos[:, None] - offsets[None, :] >= 0
    is_valid = first_ok[:, None, None, None, :] & second_ok[:, None, None, :, None]
    scores = jnp.where(is_valid, scores, -jnp.inf)
    row_top = jnp.max(scores, axis=(3, 4), keepdims=True)
    row_weights = jnp.exp(scores - row_top)
    row_sum = jnp.sum(row_weights, axis=(3, 4))
    weights_bf = row_weights.astype(jnp.bfloat16)
    first_mix = jnp.einsum(
        "ivgtj,jvd->ivgtd", weights_bf, first_vals, preferred_element_type=jnp.float32
    )
    second_side = jnp.transpose(second_vwin, (0, 2, 1, 3)).astype(jnp.float32)[:, :, None]
    combined = jnp.sum(first_mix * second_side, axis=3)
    return (combined / row_sum[..., None]).astype(jnp.bfloat16)


def on_device(
    queries, first_pair_keys, first_pair_values, second_pair_keys, second_pair_values, out_weight
):
    local_rows = queries.shape[0]
    kv_local = first_pair_keys.shape[1] // HEAD_SIZE
    seq_index = lax.axis_index("seq")
    hop_count = FIRST_WINDOW // local_rows
    key_pair = jnp.stack([first_pair_keys, first_pair_values])
    earlier = []
    moving = key_pair
    for hop_step in range(hop_count):
        moving = passed_along(moving, "seq", 1)
        earlier.insert(0, moving)
    window_pair = jnp.concatenate(earlier + [key_pair], axis=1)
    tail_start = local_rows - SECOND_WINDOW + 1
    edge_pair = passed_along(
        jnp.stack([second_pair_keys[tail_start:], second_pair_values[tail_start:]]), "seq", 1
    )
    near_pair = jnp.concatenate(
        [edge_pair, jnp.stack([second_pair_keys, second_pair_values])], axis=1
    )
    window_keys = window_pair[0].reshape(-1, kv_local, HEAD_SIZE)
    window_values = window_pair[1].reshape(-1, kv_local, HEAD_SIZE)
    near_keys = near_pair[0].reshape(-1, kv_local, HEAD_SIZE)
    near_values = near_pair[1].reshape(-1, kv_local, HEAD_SIZE)
    query_head_count = queries.reshape(local_rows, kv_local, GROUP_QUERIES, HEAD_SIZE)
    block_rows = math.gcd(64, local_rows)
    outputs = []
    for block_index in range(local_rows // block_rows):
        block_start = block_index * block_rows
        query_rows = query_head_count[block_start : block_start + block_rows]
        first_rows = window_keys[block_start : block_start + block_rows + FIRST_WINDOW]
        first_vals = window_values[block_start : block_start + block_rows + FIRST_WINDOW]
        near_k = near_keys[block_start : block_start + block_rows + SECOND_WINDOW - 1]
        near_v = near_values[block_start : block_start + block_rows + SECOND_WINDOW - 1]
        second_win = jnp.stack(
            [
                near_k[SECOND_WINDOW - 1 - lag_step : SECOND_WINDOW - 1 - lag_step + block_rows]
                for lag_step in range(SECOND_WINDOW)
            ],
            axis=1,
        )
        second_vwin = jnp.stack(
            [
                near_v[SECOND_WINDOW - 1 - lag_step : SECOND_WINDOW - 1 - lag_step + block_rows]
                for lag_step in range(SECOND_WINDOW)
            ],
            axis=1,
        )
        query_first = seq_index * local_rows + block_start
        query_pos = query_first + jnp.arange(block_rows, dtype=jnp.int32)
        key_pos = (
            query_first - FIRST_WINDOW + jnp.arange(block_rows + FIRST_WINDOW, dtype=jnp.int32)
        )
        outputs.append(
            attend_block(
                query_rows, first_rows, first_vals, second_win, second_vwin, query_pos, key_pos
            )
        )
    attended = jnp.concatenate(outputs, axis=0).reshape(
        local_rows, kv_local * GROUP_QUERIES * HEAD_SIZE
    )
    all_heads = lax.all_gather(attended, "head", axis=1, tiled=True)
    projected = jnp.dot(
        all_heads,
        lax.all_gather(out_weight, "seq", axis=0, tiled=True),
        preferred_element_type=jnp.float32,
    )
    return (attended, projected.astype(jnp.bfloat16))


def solution(mesh):
    return jax.shard_map(
        on_device,
        mesh=mesh,
        in_specs=(
            P("seq", "head"),
            P("seq", "head"),
            P("seq", "head"),
            P("seq", "head"),
            P("seq", "head"),
            P("seq", "head"),
        ),
        out_specs=(P("seq", "head"), P("seq", "head")),
        check_vma=False,
    )
```

profile of v0, /device:TPU:4, one launch (start us, length us, event | category | flops | bytes accessed | tf_op | source)
XLA Modules:
  0.0 251.5 jit_solution(15957414984685423413)
XLA Ops:
  8.0 4.3 %collective-permute-start.2 = (bf16[2,31,128]{2,1,0:T(8,128)(2,1)S(1)}, bf16[2,31,128]{2,1,0:T(8,128)(2,1)S(1)}, u32[]{:S(2)}, u32[]{:S(2)}) collective-permute-start(bf16[2,31,128]{2,1,0:T(8,128)(2,1)S(1)} %pad_maximum_fusion.1), channel_id=1, source_target_pairs={{0,8},{8,16},{16,24},{24,32},{32,40},{40,48},{48,56},{56,64},{64,7... | collective-permute-start | bytes 47624 | tf_op jit(solution)/shard_map/ppermute | solution.py:17
  12.2 1.5 pad_maximum_fusion
  13.8 4.9 %collective-permute-start = (bf16[2,256,128]{2,1,0:T(8,128)(2,1)}, bf16[2,256,128]{2,1,0:T(8,128)(2,1)}, u32[]{:S(2)}, u32[]{:S(2)}) collective-permute-start(bf16[2,256,128]{2,1,0:T(8,128)(2,1)} %pad_maximum_fusion), channel_id=1, source_target_pairs={{0,8},{8,16},{16,24},{24,32},{32,40},{40,48},{48,56},{56,64},{64,7... | collective-permute-start | bytes 393224 | tf_op jit(solution)/shard_map/ppermute | solution.py:17
  22.9 1.4 constant_dynamic-update-slice_fusion.254
  24.4 1.4 constant_dynamic-update-slice_fusion.253
  25.8 1.4 constant_dynamic-update-slice_fusion.252
  27.2 1.4 constant_dynamic-update-slice_fusion.251
  28.6 1.4 constant_dynamic-update-slice_fusion.250
  30.0 1.4 constant_dynamic-update-slice_fusion.249
  31.5 1.4 constant_dynamic-update-slice_fusion.248
  34.2 1.4 constant_dynamic-update-slice_fusion.246
  35.7 1.4 constant_dynamic-update-slice_fusion.245
  37.1 1.4 constant_dynamic-update-slice_fusion.244
  38.5 1.4 constant_dynamic-update-slice_fusion.243
  39.9 1.4 constant_dynamic-update-slice_fusion.242
  41.3 1.4 constant_dynamic-update-slice_fusion.241
  42.7 1.4 constant_dynamic-update-slice_fusion.240
  45.5 1.4 constant_dynamic-update-slice_fusion.238
  46.9 1.4 constant_dynamic-update-slice_fusion.237
  48.4 1.4 constant_dynamic-update-slice_fusion.236
  49.8 1.4 constant_dynamic-update-slice_fusion.235
  51.2 1.4 constant_dynamic-update-slice_fusion.234
  52.6 1.4 constant_dynamic-update-slice_fusion.233
  56.8 1.4 constant_dynamic-update-slice_fusion.230
  58.2 1.4 constant_dynamic-update-slice_fusion.229
  59.7 1.4 constant_dynamic-update-slice_fusion.228
  61.1 1.4 constant_dynamic-update-slice_fusion.227
  62.5 1.4 constant_dynamic-update-slice_fusion.226
  63.9 1.4 constant_dynamic-update-slice_fusion.225
  65.3 1.4 constant_dynamic-update-slice_fusion.224
  72.1 1.4 bitcast_convert_fusion
  77.1 3.7 %collective-permute-start.1 = (bf16[2,256,128]{2,1,0:T(8,128)(2,1)}, bf16[2,256,128]{2,1,0:T(8,128)(2,1)S(1)}, u32[]{:S(2)}, u32[]{:S(2)}) collective-permute-start(bf16[2,256,128]{2,1,0:T(8,128)(2,1)} %collective-permute-done), channel_id=1, source_target_pairs={{0,8},{8,16},{16,24},{24,32},{32,40},{40,48},{48,56},{56,64},{64,7... | collective-permute-start | bytes 393224 | tf_op jit(solution)/shard_map/ppermute | solution.py:17
  80.9 2.7 %collective-permute-done.1 = bf16[2,256,128]{2,1,0:T(8,128)(2,1)S(1)} collective-permute-done((bf16[2,256,128]{2,1,0:T(8,128)(2,1)}, bf16[2,256,128]{2,1,0:T(8,128)(2,1)S(1)}, u32[]{:S(2)}, u32[]{:S(2)}) %collective-permute-start.1) | collective-permute-done | bytes 131104 | tf_op jit(solution)/shard_map/ppermute | solution.py:17
  84.5 2.1 fusion.8
  86.6 4.2 %fusion = (f32[64,2]{0,1:T(2,128)S(1)}, bf16[64,2,32,576]{3,0,1,2:T(8,128)(2,1)S(1)}) fusion(f32[576,64,32,2]{0,1,3,2:T(8,128)S(1)} %get-tuple-element.209, f32[64,2]{0,1:T(2,128)S(1)} %get-tuple-element.208, pred[64,32,576]{2,0,1:T(8,128)(4,1)S(1)} %broadcast_and_fusion.3), kind=kLoop, calls=%fused_computation.8 | loop fusion | flops 11796352 | bytes 15336448 | tf_op jit(solution)/shard_map/reduce_sum | solution.py:37
  90.8 1.5 fusion.27
  92.4 2.1 fusion.9
  94.5 4.0 %fusion.2 = (f32[64,2]{0,1:T(2,128)S(1)}, bf16[64,2,32,576]{3,0,1,2:T(8,128)(2,1)S(1)}) fusion(f32[576,64,32,2]{0,1,3,2:T(8,128)S(1)} %get-tuple-element.211, f32[64,2]{0,1:T(2,128)S(1)} %get-tuple-element.210, pred[64,32,576]{2,0,1:T(8,128)(4,1)S(1)} %broadcast_and_fusion.2), kind=kLoop, calls=%fused_computation.10 | loop fusion | flops 11796352 | bytes 15336448 | tf_op jit(solution)/shard_map/reduce_sum | solution.py:37
  98.5 1.5 fusion.26
  100.1 2.1 fusion.10
  102.1 4.2 %fusion.4 = (f32[64,2]{0,1:T(2,128)S(1)}, bf16[64,2,32,576]{3,0,1,2:T(8,128)(2,1)S(1)}) fusion(f32[576,64,32,2]{0,1,3,2:T(8,128)S(1)} %get-tuple-element.213, f32[64,2]{0,1:T(2,128)S(1)} %get-tuple-element.212, pred[64,32,576]{2,0,1:T(8,128)(4,1)S(1)} %broadcast_and_fusion.1), kind=kLoop, calls=%fused_computation.12 | loop fusion | flops 11796352 | bytes 15336448 | tf_op jit(solution)/shard_map/reduce_sum | solution.py:37
  106.4 1.5 fusion.25
  107.9 2.1 fusion.11
  110.0 4.0 %fusion.6 = (f32[64,2]{0,1:T(2,128)S(1)}, bf16[64,2,32,576]{3,0,1,2:T(8,128)(2,1)S(1)}) fusion(f32[576,64,32,2]{0,1,3,2:T(8,128)S(1)} %get-tuple-element.215, f32[64,2]{0,1:T(2,128)S(1)} %get-tuple-element.214, pred[64,32,576]{2,0,1:T(8,128)(4,1)S(1)} %broadcast_and_fusion), kind=kLoop, calls=%fused_computation.14 | loop fusion | flops 11796352 | bytes 15336448 | tf_op jit(solution)/shard_map/reduce_sum | solution.py:37
  114.0 1.5 fusion.24
  117.2 31.6 %all-gather.3.cloned.1.call-done = bf16[256,2048]{1,0:T(8,128)(2,1)} async-done(((bf16[256,256]{1,0:T(8,128)(2,1)}), bf16[256,2048]{1,0:T(8,128)(2,1)}) %all-gather.3.cloned.1.call-update) | async-done | bytes 1048592 | tf_op jit(solution)/shard_map/all_gather | solution.py:109
  148.9 91.2 %all-gather.5.cloned.1.call-done = bf16[2048,1024]{1,0:T(8,128)(2,1)} async-done(((bf16[32,1024]{1,0:T(8,128)(2,1)}), bf16[2048,1024]{1,0:T(8,128)(2,1)}) %all-gather.5.cloned.1.call-update) | async-done | bytes 4194320 | tf_op jit(solution)/shard_map/all_gather | solution.py:112
  240.1 4.6 %convolution_convert_fusion = bf16[256,1024]{1,0:T(8,128)(2,1)} fusion(bf16[256,2048]{1,0:T(8,128)(2,1)} %all-gather.3.cloned.1.call-done, bf16[2048,1024]{1,0:T(8,128)(2,1)} %all-gather.5.cloned.1.call-done), kind=kOutput, calls=%fused_computation.48 | convolution fusion | flops 1074003968 | bytes 5767168 | tf_op jit(solution)/shard_map/dot_general | solution.py:110
  (156 shorter events, 21.6 us)
Async XLA Ops:
  7.2 141.7 %all-gather.3.cloned.1.call-start = ((), (), s32[]{:S(2)}) async-start(), calls=%async_computation | async-start | bytes 1179648 | tf_op jit(solution)/shard_map/all_gather | solution.py:109
  8.0 67.8 %collective-permute-start.2 = (bf16[2,31,128]{2,1,0:T(8,128)(2,1)S(1)}, bf16[2,31,128]{2,1,0:T(8,128)(2,1)S(1)}, u32[]{:S(2)}, u32[]{:S(2)}) collective-permute-start(bf16[2,31,128]{2,1,0:T(8,128)(2,1)S(1)} %pad_maximum_fusion.1), channel_id=1, source_target_pairs={{0,8},{8,16},{16,24},{24,32},{32,40},{40,48},{48,56},{56,64},{64,7... | collective-permute-start | bytes 47624 | tf_op jit(solution)/shard_map/ppermute | solution.py:17
  13.8 63.3 %collective-permute-start = (bf16[2,256,128]{2,1,0:T(8,128)(2,1)}, bf16[2,256,128]{2,1,0:T(8,128)(2,1)}, u32[]{:S(2)}, u32[]{:S(2)}) collective-permute-start(bf16[2,256,128]{2,1,0:T(8,128)(2,1)} %pad_maximum_fusion), channel_id=1, source_target_pairs={{0,8},{8,16},{16,24},{24,32},{32,40},{40,48},{48,56},{56,64},{64,7... | collective-permute-start | bytes 393224 | tf_op jit(solution)/shard_map/ppermute | solution.py:17
  66.8 7.7 %copy-start = (bf16[256,128]{1,0:T(8,128)(2,1)S(1)}, bf16[256,128]{1,0:T(8,128)(2,1)}, u32[]{:S(2)}) copy-start(bf16[256,128]{1,0:T(8,128)(2,1)} %param.9) | copy-start | bytes 196612
  73.5 2.2 copy-start.1
  75.3 8.3 %copy-start.2 = (bf16[256,128]{1,0:T(8,128)(2,1)S(1)}, bf16[256,128]{1,0:T(8,128)(2,1)}, u32[]{:S(2)}) copy-start(bf16[256,128]{1,0:T(8,128)(2,1)} %param.8) | copy-start | bytes 196612
  75.3 8.3 %copy-start.3 = (bf16[256,128]{1,0:T(8,128)(2,1)S(1)}, bf16[256,128]{1,0:T(8,128)(2,1)}, u32[]{:S(2)}) copy-start(bf16[256,128]{1,0:T(8,128)(2,1)} %param.7) | copy-start | bytes 196612
  77.1 6.5 %collective-permute-start.1 = (bf16[2,256,128]{2,1,0:T(8,128)(2,1)}, bf16[2,256,128]{2,1,0:T(8,128)(2,1)S(1)}, u32[]{:S(2)}, u32[]{:S(2)}) collective-permute-start(bf16[2,256,128]{2,1,0:T(8,128)(2,1)} %collective-permute-done), channel_id=1, source_target_pairs={{0,8},{8,16},{16,24},{24,32},{32,40},{40,48},{48,56},{56,64},{64,7... | collective-permute-start | bytes 393224 | tf_op jit(solution)/shard_map/ppermute | solution.py:17
  115.8 0.7 copy-start.4
  116.5 123.6 %all-gather.5.cloned.1.call-start = ((), (), s32[]{:S(2)}) async-start(), calls=%async_computation.1 | async-start | bytes 4259840 | tf_op jit(solution)/shard_map/all_gather | solution.py:112
Sparse Core Ops, SparseCore 0:
  116.6 32.2 all-gather.2
  151.9 88.1 all-gather.4
where the time goes:
time: 254 us; the launch traced here: 251 us
  waiting for transfers between devices  126 us (50%)
  local copies, waits for them, and re-layouts  49 us (19%)
  other arithmetic  29.4 us (12%)
  matrix products  18.9 us (7%)
  between operations  14.9 us (6%)
  starting transfers between devices  12.9 us (5%)
    all_gather x1, waiting for transfers between devices, on_device(): lax.all_gather(out_weight, 'seq', axis=0, tiled=True)  91.2 us
    unnamed x132, local copies, waits for them, and re-layouts  46.8 us
    all_gather x1, waiting for transfers between devices, on_device(): all_heads = lax.all_gather(attended, 'head', axis=1, tiled=True)  31.6 us
    reduce_sum x4, other arithmetic, attend_block(): row_sum = jnp.sum(row_weights, axis=(3, 4))  16.4 us
    ppermute x3, starting transfers between devices, passed_along(): return lax.ppermute(x, axis, pairs)  12.9 us
    dot_general x4, matrix products, attend_block(): jnp.einsum('itvgd,jvd->ivgtj', query_mod, first_rows, preferred_element_t...  8.26 us
    dot_general x4, matrix products, attend_block(): jnp.einsum('ivgtj,jvd->ivgtd', weights_bf, first_vals, preferred_element_...  6.14 us
  transfers between devices with their start and end apart: 5, of which 3 were waited for; matrix products, arithmetic and copies ran while one was open for 24% of the time, Pallas kernels for 0%

commit v1 on v0

v1 whole, which is shorter than its diff:
```python
import functools
import math

import jax
import jax.numpy as jnp
from jax import lax
from jax.experimental import pallas as pl
from jax.experimental.pallas import tpu as pltpu
from jax.sharding import PartitionSpec as P

HEAD = 128
GROUP = 2
FIRST = 512
SECOND = 32
ROWS = 256
BLOCK = 128
KEYS = FIRST + BLOCK
STEP = 8
SCALE = HEAD ** (-0.5) * math.log2(math.e)


def attend(b, g, index, queries, far, near, keys, values, second_keys, second_values, out, k_all, v_all, k2, v2, kept, score, total, top):
    first_block = index[0]
    base = b * BLOCK
    spare = jnp.broadcast_to(keys[0:1, :].astype(jnp.float32), (BLOCK, HEAD)).astype(jnp.bfloat16)
    zero = jnp.zeros((BLOCK, HEAD), jnp.bfloat16)
    one = jnp.ones((BLOCK, HEAD), jnp.bfloat16)

    for piece in range(KEYS // BLOCK):
        slot, at = divmod(base + piece * BLOCK, ROWS)
        to = slice(piece * BLOCK, (piece + 1) * BLOCK)
        if slot == 2:
            k_all[to, :] = keys[at : at + BLOCK, :]
            v_all[to, :HEAD] = values[at : at + BLOCK, :]
            v_all[to, HEAD:] = one
        else:
            source = (far, near)[slot]
            held = first_block >= 2 - slot
            k_all[to, :] = jnp.where(held, source[at : at + BLOCK, :], spare)
            v_all[to, :HEAD] = jnp.where(held, source[ROWS + at : ROWS + at + BLOCK, :], zero)
            v_all[to, HEAD:] = jnp.where(held, one, zero)

    if b == 0:
        held = first_block >= 1
        edge_k = near[2 * ROWS : 2 * ROWS + SECOND, :].astype(jnp.float32)
        edge_v = near[2 * ROWS + SECOND : 2 * ROWS + 2 * SECOND, :].astype(jnp.float32)
        spare2 = jnp.broadcast_to(second_keys[0:1, :].astype(jnp.float32), (SECOND, HEAD))
        kept[0, 0:SECOND, :] = jnp.where(held, edge_k, spare2)
        kept[1, 0:SECOND, :] = jnp.where(held, edge_v, jnp.zeros_like(edge_v))
        kept[2, 0:SECOND, :] = jnp.where(held, jnp.ones_like(edge_v), jnp.zeros_like(edge_v))
        kept[0, SECOND:, :] = second_keys[:BLOCK, :].astype(jnp.float32)
        kept[1, SECOND:, :] = second_values[:BLOCK, :].astype(jnp.float32)
        kept[2, SECOND:, :] = jnp.ones((BLOCK, HEAD), jnp.float32)
    else:
        kept[0] = second_keys[base - SECOND : base + BLOCK, :].astype(jnp.float32)
        kept[1] = second_values[base - SECOND : base + BLOCK, :].astype(jnp.float32)
    for r in range(STEP):
        k2[r, STEP:, :] = kept[0, STEP - r : SECOND + BLOCK - r, :]
        v2[r, STEP:, :HEAD] = kept[1, STEP - r : SECOND + BLOCK - r, :]
        if b == 0:
            v2[r, STEP:, HEAD:] = kept[2, STEP - r : SECOND + BLOCK - r, :]
        else:
            v2[r, STEP:, HEAD:] = jnp.ones((SECOND + BLOCK - STEP, HEAD), jnp.float32)

    row = lax.broadcasted_iota(jnp.int32, (BLOCK, HEAD), 0)
    col = lax.broadcasted_iota(jnp.int32, (BLOCK, HEAD), 1)
    upper = col > row
    q = queries[base : base + BLOCK, g * HEAD : (g + 1) * HEAD].astype(jnp.float32)
    k_win = k_all[...]
    v_win = v_all[...]
    top[...] = jnp.full((BLOCK, HEAD), -1e30, jnp.float32)
    total[...] = jnp.zeros((BLOCK, 2 * HEAD), jnp.float32)

    def step(a, _):
        start = pl.multiple_of(SECOND - STEP * a, STEP)
        most = None
        for r in range(STEP):
            mod = (q * k2[r, pl.ds(start, BLOCK), :]).astype(jnp.bfloat16)
            s = lax.dot_general(mod, k_win, (((1,), (1,)), ((), ())), preferred_element_type=jnp.float32)
            edge = jnp.where(upper, s[:, :HEAD], s[:, FIRST:])
            score[r, :, :HEAD] = edge
            score[r, :, HEAD:] = s[:, HEAD:FIRST]
            here = jnp.maximum(
                jnp.maximum(edge, s[:, HEAD : 2 * HEAD]),
                jnp.maximum(s[:, 2 * HEAD : 3 * HEAD], s[:, 3 * HEAD : FIRST]),
            )
            most = here if most is None else jnp.maximum(most, here)
        old = top[...]
        new = jnp.maximum(old, jnp.max(most, axis=1, keepdims=True))
        top[...] = new
        shift = new * SCALE
        shrink = jnp.exp2(old * SCALE - shift)
        acc = total[...] * jnp.concatenate([shrink, shrink], axis=1)
        for r in range(STEP):
            parts = [
                jnp.exp2(score[r, :, k * HEAD : (k + 1) * HEAD] * SCALE - shift) for k in range(FIRST // HEAD)
            ]
            nothing = jnp.zeros_like(parts[0])
            ends = [jnp.where(upper, parts[0], nothing), jnp.where(upper, nothing, parts[0])]
            weights = jnp.concatenate(ends[:1] + parts[1:] + ends[1:], axis=1).astype(jnp.bfloat16)
            mix = jnp.dot(weights, v_win, preferred_element_type=jnp.float32)
            acc = acc + mix * v2[r, pl.ds(start, BLOCK), :]
        total[...] = acc
        return 0

    lax.fori_loop(0, SECOND // STEP, step, 0)
    out[...] = (total[:, :HEAD] / total[:, HEAD:]).astype(jnp.bfloat16)


def attention(b, g, *operands):
    vmem = pl.BlockSpec(memory_space=pltpu.VMEM)
    return pl.pallas_call(
        functools.partial(attend, b, g),
        out_shape=jax.ShapeDtypeStruct((BLOCK, HEAD), jnp.bfloat16),
        in_specs=[pl.BlockSpec(memory_space=pltpu.SMEM)] + [vmem] * 7,
        out_specs=vmem,
        scratch_shapes=[
            pltpu.VMEM((KEYS, HEAD), jnp.bfloat16),
            pltpu.VMEM((KEYS, 2 * HEAD), jnp.bfloat16),
            pltpu.VMEM((STEP, BLOCK + SECOND, HEAD), jnp.float32),
            pltpu.VMEM((STEP, BLOCK + SECOND, 2 * HEAD), jnp.float32),
            pltpu.VMEM((3, BLOCK + SECOND, HEAD), jnp.float32),
            pltpu.VMEM((STEP, BLOCK, FIRST), jnp.float32),
            pltpu.VMEM((BLOCK, 2 * HEAD), jnp.float32),
            pltpu.VMEM((BLOCK, HEAD), jnp.float32),
        ],
        compiler_params=pltpu.CompilerParams(vmem_limit_bytes=24 * 1024 * 1024),
        cost_estimate=pl.CostEstimate(flops=3_000_000_000, bytes_accessed=1_000_000, transcendentals=3_000_000),
        name="attend",
    )(*operands)


def project(order, direct, swapped, weight, out, total):
    for k in range(SIDE):
        at = order[k]
        rows = jnp.where(order[SIDE + k] == 0, direct[at], swapped[at])
        piece = jnp.dot(rows, weight[k], preferred_element_type=jnp.float32)
        if k == 0:
            total[...] = piece
        elif k < SIDE - 1:
            total[...] += piece
        else:
            out[...] = (total[...] + piece).astype(jnp.bfloat16)


def projection(order, direct, swapped, weight):
    width = weight.shape[-1]
    vmem = pl.BlockSpec(memory_space=pltpu.VMEM)
    return pl.pallas_call(
        project,
        out_shape=jax.ShapeDtypeStruct((ROWS, width), jnp.bfloat16),
        in_specs=[pl.BlockSpec(memory_space=pltpu.SMEM)] + [vmem] * 3,
        out_specs=vmem,
        scratch_shapes=[pltpu.VMEM((ROWS, width), jnp.float32)],
        compiler_params=pltpu.CompilerParams(vmem_limit_bytes=24 * 1024 * 1024),
        cost_estimate=pl.CostEstimate(flops=1_100_000_000, bytes_accessed=6_000_000, transcendentals=0),
        name="project",
    )(order, direct, swapped, weight)


SIDE = 8
CHIPS = 4
HOPS = (0, 1, 3, 2)


def shifted(x, by):
    size = lax.axis_size("seq")
    return lax.ppermute(x, "seq", [(i, i + by) for i in range(size - by)])


def on_device(queries, first_keys, first_values, second_keys, second_values, out_weight):
    width = out_weight.shape[1]
    packed = jnp.concatenate([first_keys, first_values, second_keys[-SECOND:], second_values[-SECOND:]], axis=0)
    near = shifted(packed, 1)
    far = shifted(packed, 2)
    weight = lax.all_gather(out_weight, "seq", axis=0, tiled=True).reshape(SIDE, ROWS, width)
    seq = lax.axis_index("seq").astype(jnp.int32)
    head = lax.axis_index("head").astype(jnp.int32)
    operands = (seq.reshape(1), queries, far, near, first_keys, first_values, second_keys, second_values)
    pieces = [attention(b, g, *operands) for b in range(ROWS // BLOCK) for g in range(GROUP)]
    attended = jnp.concatenate(
        [jnp.concatenate(pieces[:2], axis=1), jnp.concatenate(pieces[2:], axis=1)], axis=0
    )
    direct = [attended]
    for hop in HOPS[1:]:
        pairs = [(2 * x + c, 2 * ((x + hop) % CHIPS) + c) for x in range(CHIPS) for c in range(2)]
        direct.append(lax.ppermute(attended, "head", pairs))
    direct = jnp.stack(direct)
    swapped = lax.ppermute(direct, "head", [(2 * x + c, 2 * x + 1 - c) for x in range(CHIPS) for c in range(2)])
    chip, core = lax.div(head, 2), lax.rem(head, 2)
    owner = jnp.arange(SIDE, dtype=jnp.int32)
    distance = lax.rem(chip - lax.div(owner, 2) + CHIPS, CHIPS)
    place = jnp.where(distance < 2, distance, 5 - distance)
    part = jnp.where(lax.rem(owner, 2) == core, 0, 1)
    order = jnp.concatenate([place, part]).astype(jnp.int32)
    return attended, projection(order, direct, swapped, weight)


def solution(mesh):
    spec = P("seq", "head")
    return jax.shard_map(on_device, mesh=mesh, in_specs=(spec,) * 6, out_specs=(spec, spec), check_vma=False)
```

time: 254 us -> 115 us (0.45)
  the two profiles are of different devices: /device:TPU:4 before, /device:TPU:2 now
where the time goes in v1:
time: 115 us; the launch traced here: 114 us
  waiting for transfers between devices  40.2 us (35%)
  Pallas kernels  28.7 us (25%)
  starting transfers between devices  22.2 us (19%)
  between operations  14.2 us (12%)
  local copies, waits for them, and re-layouts  7.85 us (7%)
    all_gather x1, waiting for transfers between devices, on_device(): lax.all_gather(out_weight, 'seq', axis=0, tiled=True)  30.6 us
    pallas_call x4, Pallas kernels, attention(): pl.pallas_call(functools.partial(attend, b, g), out_shape=jax.ShapeDtypeS...  26.1 us
    ppermute x2, starting transfers between devices, shifted(): return lax.ppermute(x, 'seq', [(i, i + by) for i in range(size - by)])  10.4 us
    ppermute x3, starting transfers between devices, on_device(): direct.append(lax.ppermute(attended, 'head', pairs))  9.88 us
    unnamed x14, local copies, waits for them, and re-layouts  6.45 us
    ppermute x3, waiting for transfers between devices, on_device(): direct.append(lax.ppermute(attended, 'head', pairs))  4.33 us
    ppermute x2, waiting for transfers between devices, shifted(): return lax.ppermute(x, 'seq', [(i, i + by) for i in range(size - by)])  2.79 us
    pallas_call x1, Pallas kernels, projection(): pl.pallas_call(project, out_shape=jax.ShapeDtypeStruct((ROWS, width), jnp...  2.61 us
  transfers between devices with their start and end apart: 7, of which 5 were waited for; matrix products, arithmetic and copies ran while one was open for 2% of the time, Pallas kernels for 23%

profile of v1, /device:TPU:2, one launch (start us, length us, event | category | flops | bytes accessed | tf_op | source)
XLA Modules:
  0.0 114.2 jit_solution(10718485251976105262)
XLA Ops:
  7.2 0.0 all-gather.2.cloned.1.call-start
  7.2 0.7 all-gather.2.cloned.1.call-update
  7.9 0.7 slice.6
  8.6 0.7 slice.7
  9.3 0.9 pad_maximum_fusion.1
  10.2 4.3 %collective-permute-start.1 = (bf16[576,128]{1,0:T(8,128)(2,1)S(1)}, bf16[576,128]{1,0:T(8,128)(2,1)S(1)}, u32[]{:S(2)}, u32[]{:S(2)}) collective-permute-start(bf16[576,128]{1,0:T(8,128)(2,1)S(1)} %pad_maximum_fusion.1), channel_id=1, source_target_pairs={{0,8},{8,16},{16,24},{24,32},{32,40},{40,48},{48,56},{56,64},{64,7... | collective-permute-start | bytes 442376 | tf_op jit(solution)/shard_map/ppermute | solution.py:168
  14.5 6.1 %collective-permute-start = (bf16[576,128]{1,0:T(8,128)(2,1)S(1)}, bf16[576,128]{1,0:T(8,128)(2,1)S(1)}, u32[]{:S(2)}, u32[]{:S(2)}) collective-permute-start(bf16[576,128]{1,0:T(8,128)(2,1)S(1)} %pad_maximum_fusion.1), channel_id=1, source_target_pairs={{0,16},{8,24},{16,32},{24,40},{32,48},{40,56},{48,64},{56,72},{64,... | collective-permute-start | bytes 442376 | tf_op jit(solution)/shard_map/ppermute | solution.py:168
  20.6 0.0 collective-permute-done.1.near
  20.6 2.8 %collective-permute-done.far = bf16[576,128]{1,0:T(8,128)(2,1)S(1)} collective-permute-done((bf16[576,128]{1,0:T(8,128)(2,1)S(1)}, bf16[576,128]{1,0:T(8,128)(2,1)S(1)}, u32[]{:S(2)}, u32[]{:S(2)}) %collective-permute-start) | collective-permute-done | bytes 147488 | tf_op jit(solution)/shard_map/ppermute | solution.py:168
  23.4 0.0 copy-start.1
  23.4 0.8 copy-done.1
  24.2 0.0 copy-start.2
  24.2 0.8 copy-done.2
  25.1 0.0 copy-start.3
  25.1 0.8 copy-done.3
  25.9 0.0 copy-start.4
  25.9 0.8 copy-done.4
  26.7 0.0 copy-start.5
  26.7 0.9 copy-done.5
  27.6 6.5 %attend.7 = bf16[128,128]{1,0:T(8,128)(2,1)S(1)} custom-call(s32[1]{0:T(128)} %bitcast.index, bf16[256,256]{1,0:T(8,128)(2,1)S(1)} %copy-done.5, bf16[576,128]{1,0:T(8,128)(2,1)S(1)} %collective-permute-done.far, bf16[576,128]{1,0:T(8,128)(2,1)S(1)} %collective-permute-done.1.near, bf16[256,128]{1,0:T(8,128)(2,1)S(1)} %copy-done.2, ...), custom_call_target="tpu_custom_call" | custom-call | flops 3000000000 | bytes 1000000 | tf_op jit(solution)/shard_map/attend/pallas_call | solution.py:112
  34.1 6.5 %attend.6 = bf16[128,128]{1,0:T(8,128)(2,1)S(1)} custom-call(s32[1]{0:T(128)} %bitcast.index, bf16[256,256]{1,0:T(8,128)(2,1)S(1)} %copy-done.5, bf16[576,128]{1,0:T(8,128)(2,1)S(1)} %collective-permute-done.far, bf16[576,128]{1,0:T(8,128)(2,1)S(1)} %collective-permute-done.1.near, bf16[256,128]{1,0:T(8,128)(2,1)S(1)} %copy-done.2, ...), custom_call_target="tpu_custom_call" | custom-call | flops 3000000000 | bytes 1000000 | tf_op jit(solution)/shard_map/attend/pallas_call | solution.py:112
  40.7 6.5 %attend.5 = bf16[128,128]{1,0:T(8,128)(2,1)S(1)} custom-call(s32[1]{0:T(128)} %bitcast.index, bf16[256,256]{1,0:T(8,128)(2,1)S(1)} %copy-done.5, bf16[576,128]{1,0:T(8,128)(2,1)S(1)} %collective-permute-done.far, bf16[576,128]{1,0:T(8,128)(2,1)S(1)} %collective-permute-done.1.near, bf16[256,128]{1,0:T(8,128)(2,1)S(1)} %copy-done.2, ...), custom_call_target="tpu_custom_call" | custom-call | flops 3000000000 | bytes 1000000 | tf_op jit(solution)/shard_map/attend/pallas_call | solution.py:112
  47.2 6.5 %attend.4 = bf16[128,128]{1,0:T(8,128)(2,1)S(1)} custom-call(s32[1]{0:T(128)} %bitcast.index, bf16[256,256]{1,0:T(8,128)(2,1)S(1)} %copy-done.5, bf16[576,128]{1,0:T(8,128)(2,1)S(1)} %collective-permute-done.far, bf16[576,128]{1,0:T(8,128)(2,1)S(1)} %collective-permute-done.1.near, bf16[256,128]{1,0:T(8,128)(2,1)S(1)} %copy-done.2, ...), custom_call_target="tpu_custom_call" | custom-call | flops 3000000000 | bytes 1000000 | tf_op jit(solution)/shard_map/attend/pallas_call | solution.py:112
  53.8 0.0 copy-start.6
  53.8 4.0 %collective-permute-start.4 = (bf16[256,256]{1,0:T(8,128)(2,1)S(1)}, bf16[256,256]{1,0:T(8,128)(2,1)S(1)}, u32[]{:S(2)}, u32[]{:S(2)}) collective-permute-start(bf16[256,256]{1,0:T(8,128)(2,1)S(1)} %maximum_maximum_fusion), channel_id=1, source_target_pairs={{0,4},{1,5},{2,6},{3,7},{4,0},{5,1},{6,2},{7,3},{8,12},{9,13},{10,... | collective-permute-start | bytes 393224 | tf_op jit(solution)/shard_map/ppermute | solution.py:187
  57.8 3.4 %collective-permute-start.3 = (bf16[256,256]{1,0:T(8,128)(2,1)S(1)}, bf16[256,256]{1,0:T(8,128)(2,1)S(1)}, u32[]{:S(2)}, u32[]{:S(2)}) collective-permute-start(bf16[256,256]{1,0:T(8,128)(2,1)S(1)} %maximum_maximum_fusion), channel_id=1, source_target_pairs={{0,6},{1,7},{2,0},{3,1},{4,2},{5,3},{6,4},{7,5},{8,14},{9,15},{10,... | collective-permute-start | bytes 393224 | tf_op jit(solution)/shard_map/ppermute | solution.py:187
  61.2 2.5 %collective-permute-start.2 = (bf16[256,256]{1,0:T(8,128)(2,1)S(1)}, bf16[256,256]{1,0:T(8,128)(2,1)S(1)}, u32[]{:S(2)}, u32[]{:S(2)}) collective-permute-start(bf16[256,256]{1,0:T(8,128)(2,1)S(1)} %maximum_maximum_fusion), channel_id=1, source_target_pairs={{0,2},{1,3},{2,4},{3,5},{4,6},{5,7},{6,0},{7,1},{8,10},{9,11},{10,... | collective-permute-start | bytes 393224 | tf_op jit(solution)/shard_map/ppermute | solution.py:187
  63.7 0.0 collective-permute-done.4
  63.7 1.1 collective-permute-done.3
  64.8 3.2 %collective-permute-done.2 = bf16[256,256]{1,0:T(8,128)(2,1)S(1)} collective-permute-done((bf16[256,256]{1,0:T(8,128)(2,1)S(1)}, bf16[256,256]{1,0:T(8,128)(2,1)S(1)}, u32[]{:S(2)}, u32[]{:S(2)}) %collective-permute-start.2) | collective-permute-done | bytes 131104 | tf_op jit(solution)/shard_map/ppermute | solution.py:187
  68.1 0.1 pad_maximum_fusion.direct
  68.1 1.9 %collective-permute-start.5 = (bf16[4,256,256]{2,1,0:T(8,128)(2,1)S(1)}, bf16[4,256,256]{2,1,0:T(8,128)(2,1)S(1)}, u32[]{:S(2)}, u32[]{:S(2)}) collective-permute-start(bf16[4,256,256]{2,1,0:T(8,128)(2,1)S(1)} %pad_maximum_fusion.direct), channel_id=1, source_target_pairs={{0,1},{1,0},{2,3},{3,2},{4,5},{5,4},{6,7},{7,6},{8,9},{9,8},{10,11... | collective-permute-start | bytes 1572872 | tf_op jit(solution)/shard_map/ppermute | solution.py:189
  70.1 0.1 pad_add_fusion.order
  70.1 1.8 %collective-permute-done.5.swapped = bf16[4,256,256]{2,1,0:T(8,128)(2,1)S(1)} collective-permute-done((bf16[4,256,256]{2,1,0:T(8,128)(2,1)S(1)}, bf16[4,256,256]{2,1,0:T(8,128)(2,1)S(1)}, u32[]{:S(2)}, u32[]{:S(2)}) %collective-permute-start.5) | collective-permute-done | bytes 524320 | tf_op jit(solution)/shard_map/ppermute | solution.py:189
  71.9 30.6 %all-gather.2.cloned.1.call-done = bf16[2048,1024]{1,0:T(8,128)(2,1)} async-done(((bf16[32,1024]{1,0:T(8,128)(2,1)}), bf16[2048,1024]{1,0:T(8,128)(2,1)}) %all-gather.2.cloned.1.call-update) | async-done | bytes 4194320 | tf_op jit(solution)/shard_map/all_gather | solution.py:176
  102.5 0.0 copy-start
  102.5 2.2 %copy-done = bf16[2048,1024]{1,0:T(8,128)(2,1)S(1)} copy-done((bf16[2048,1024]{1,0:T(8,128)(2,1)S(1)}, bf16[2048,1024]{1,0:T(8,128)(2,1)}, u32[]{:S(2)}) %copy-start) | copy-done | bytes 4194328
  104.7 2.6 %project.1 = bf16[256,1024]{1,0:T(8,128)(2,1)} custom-call(s32[16]{0:T(128)S(1)} %pad_add_fusion.order, bf16[4,256,256]{2,1,0:T(8,128)(2,1)S(1)} %pad_maximum_fusion.direct, bf16[4,256,256]{2,1,0:T(8,128)(2,1)S(1)} %collective-permute-done.5.swapped, bf16[8,256,1024]{2,1,0:T(8,128)(2,1)S(1)} %bitcast.7), custom_call_target="tpu_custom_call" | custom-call | flops 1100000000 | bytes 6000000 | tf_op jit(solution)/shard_map/project/pallas_call | solution.py:149
  107.3 0.0 copy-done.6
  (3 shorter events, 0.0 us)
Async XLA Ops:
  7.2 95.4 %all-gather.2.cloned.1.call-start = ((), (), s32[]{:S(2)}) async-start(), calls=%async_computation | async-start | bytes 4259840 | tf_op jit(solution)/shard_map/all_gather | solution.py:176
  10.2 10.4 %collective-permute-start.1 = (bf16[576,128]{1,0:T(8,128)(2,1)S(1)}, bf16[576,128]{1,0:T(8,128)(2,1)S(1)}, u32[]{:S(2)}, u32[]{:S(2)}) collective-permute-start(bf16[576,128]{1,0:T(8,128)(2,1)S(1)} %pad_maximum_fusion.1), channel_id=1, source_target_pairs={{0,8},{8,16},{16,24},{24,32},{32,40},{40,48},{48,56},{56,64},{64,7... | collective-permute-start | bytes 442376 | tf_op jit(solution)/shard_map/ppermute | solution.py:168
  14.5 8.9 %collective-permute-start = (bf16[576,128]{1,0:T(8,128)(2,1)S(1)}, bf16[576,128]{1,0:T(8,128)(2,1)S(1)}, u32[]{:S(2)}, u32[]{:S(2)}) collective-permute-start(bf16[576,128]{1,0:T(8,128)(2,1)S(1)} %pad_maximum_fusion.1), channel_id=1, source_target_pairs={{0,16},{8,24},{16,32},{24,40},{32,48},{40,56},{48,64},{56,72},{64,... | collective-permute-start | bytes 442376 | tf_op jit(solution)/shard_map/ppermute | solution.py:168
  23.4 0.8 copy-start.1
  24.2 0.8 copy-start.2
  25.1 0.8 copy-start.3
  25.9 0.8 copy-start.4
  26.7 0.9 copy-start.5
  53.8 53.6 %copy-start.6 = (bf16[256,256]{1,0:T(8,128)(2,1)}, bf16[256,256]{1,0:T(8,128)(2,1)S(1)}, u32[]{:S(2)}) copy-start(bf16[256,256]{1,0:T(8,128)(2,1)S(1)} %maximum_maximum_fusion) | copy-start | bytes 393220
  53.8 9.9 %collective-permute-start.4 = (bf16[256,256]{1,0:T(8,128)(2,1)S(1)}, bf16[256,256]{1,0:T(8,128)(2,1)S(1)}, u32[]{:S(2)}, u32[]{:S(2)}) collective-permute-start(bf16[256,256]{1,0:T(8,128)(2,1)S(1)} %maximum_maximum_fusion), channel_id=1, source_target_pairs={{0,4},{1,5},{2,6},{3,7},{4,0},{5,1},{6,2},{7,3},{8,12},{9,13},{10,... | collective-permute-start | bytes 393224 | tf_op jit(solution)/shard_map/ppermute | solution.py:187
  57.8 7.0 %collective-permute-start.3 = (bf16[256,256]{1,0:T(8,128)(2,1)S(1)}, bf16[256,256]{1,0:T(8,128)(2,1)S(1)}, u32[]{:S(2)}, u32[]{:S(2)}) collective-permute-start(bf16[256,256]{1,0:T(8,128)(2,1)S(1)} %maximum_maximum_fusion), channel_id=1, source_target_pairs={{0,6},{1,7},{2,0},{3,1},{4,2},{5,3},{6,4},{7,5},{8,14},{9,15},{10,... | collective-permute-start | bytes 393224 | tf_op jit(solution)/shard_map/ppermute | solution.py:187
  61.2 6.9 %collective-permute-start.2 = (bf16[256,256]{1,0:T(8,128)(2,1)S(1)}, bf16[256,256]{1,0:T(8,128)(2,1)S(1)}, u32[]{:S(2)}, u32[]{:S(2)}) collective-permute-start(bf16[256,256]{1,0:T(8,128)(2,1)S(1)} %maximum_maximum_fusion), channel_id=1, source_target_pairs={{0,2},{1,3},{2,4},{3,5},{4,6},{5,7},{6,0},{7,1},{8,10},{9,11},{10,... | collective-permute-start | bytes 393224 | tf_op jit(solution)/shard_map/ppermute | solution.py:187
  68.1 3.8 %collective-permute-start.5 = (bf16[4,256,256]{2,1,0:T(8,128)(2,1)S(1)}, bf16[4,256,256]{2,1,0:T(8,128)(2,1)S(1)}, u32[]{:S(2)}, u32[]{:S(2)}) collective-permute-start(bf16[4,256,256]{2,1,0:T(8,128)(2,1)S(1)} %pad_maximum_fusion.direct), channel_id=1, source_target_pairs={{0,1},{1,0},{2,3},{3,2},{4,5},{5,4},{6,7},{7,6},{8,9},{9,8},{10,11... | collective-permute-start | bytes 1572872 | tf_op jit(solution)/shard_map/ppermute | solution.py:189
  102.5 2.2 %copy-start = (bf16[2048,1024]{1,0:T(8,128)(2,1)S(1)}, bf16[2048,1024]{1,0:T(8,128)(2,1)}, u32[]{:S(2)}) copy-start(bf16[2048,1024]{1,0:T(8,128)(2,1)} %all-gather.2.cloned.1.call-done) | copy-start | bytes 12582916
Sparse Core Ops, SparseCore 0:
  11.0 91.5 all-gather.1

commit v2 on v1

v2 whole, which is shorter than its diff:
```python
import math

import jax
import jax.numpy as jnp
from jax import lax
from jax.experimental import pallas as pl
from jax.experimental.pallas import tpu as pltpu
from jax.sharding import PartitionSpec as P


HEAD = 128
GROUP = 2
FIRST = 512
SECOND = 32
ROWS = 256
BLOCK = 128
KEYS = FIRST + BLOCK
STEP = 8
SCALE = HEAD ** (-0.5) * math.log2(math.e)


def attend(index, *refs):
    sources, out, held_refs, sems = refs[:7], refs[7], refs[8:15], refs[15]
    k_all, v_all, k2, v2, kept, score, total, top = refs[16:]
    moves = [pltpu.make_async_copy(src, dst, sems.at[i]) for i, (src, dst) in enumerate(zip(sources, held_refs))]
    for move in moves:
        move.start()
    for move in moves:
        move.wait()
    queries, far, near, keys, values, second_keys, second_values = held_refs
    first_block = index[0]
    spare = jnp.broadcast_to(keys[0:1, :].astype(jnp.float32), (ROWS, HEAD)).astype(jnp.bfloat16)
    zero = jnp.zeros((ROWS, HEAD), jnp.bfloat16)
    one = jnp.ones((ROWS, HEAD), jnp.bfloat16)
    row = lax.broadcasted_iota(jnp.int32, (BLOCK, HEAD), 0)
    col = lax.broadcasted_iota(jnp.int32, (BLOCK, HEAD), 1)
    upper = col > row

    for slot, source in enumerate((far, near)):
        held = first_block >= 2 - slot
        to = slice(slot * ROWS, (slot + 1) * ROWS)
        k_all[to, :] = jnp.where(held, source[:ROWS, :], spare)
        v_all[to, :HEAD] = jnp.where(held, source[ROWS : 2 * ROWS, :], zero)
        v_all[to, HEAD:] = jnp.where(held, one, zero)
    k_all[2 * ROWS :, :] = keys[...]
    v_all[2 * ROWS :, :HEAD] = values[...]
    v_all[2 * ROWS :, HEAD:] = one

    for b in range(ROWS // BLOCK):
        base = b * BLOCK
        if b == 0:
            held = first_block >= 1
            edge_k = near[2 * ROWS : 2 * ROWS + SECOND, :].astype(jnp.float32)
            edge_v = near[2 * ROWS + SECOND : 2 * ROWS + 2 * SECOND, :].astype(jnp.float32)
            spare2 = jnp.broadcast_to(second_keys[0:1, :].astype(jnp.float32), (SECOND, HEAD))
            kept[0, 0:SECOND, :] = jnp.where(held, edge_k, spare2)
            kept[1, 0:SECOND, :] = jnp.where(held, edge_v, jnp.zeros_like(edge_v))
            kept[2, 0:SECOND, :] = jnp.where(held, jnp.ones_like(edge_v), jnp.zeros_like(edge_v))
            kept[0, SECOND:, :] = second_keys[:BLOCK, :].astype(jnp.float32)
            kept[1, SECOND:, :] = second_values[:BLOCK, :].astype(jnp.float32)
            kept[2, SECOND:, :] = jnp.ones((BLOCK, HEAD), jnp.float32)
        else:
            kept[0] = second_keys[base - SECOND : base + BLOCK, :].astype(jnp.float32)
            kept[1] = second_values[base - SECOND : base + BLOCK, :].astype(jnp.float32)
        for r in range(STEP):
            k2[r, STEP:, :] = kept[0, STEP - r : SECOND + BLOCK - r, :]
            v2[r, STEP:, :HEAD] = kept[1, STEP - r : SECOND + BLOCK - r, :]
            if b == 0:
                v2[r, STEP:, HEAD:] = kept[2, STEP - r : SECOND + BLOCK - r, :]
            else:
                v2[r, STEP:, HEAD:] = jnp.ones((SECOND + BLOCK - STEP, HEAD), jnp.float32)

        k_win = k_all[base : base + KEYS, :]
        v_win = v_all[base : base + KEYS, :]
        for g in range(GROUP):
            q = queries[base : base + BLOCK, g * HEAD : (g + 1) * HEAD].astype(jnp.float32)

            def scored(a, r, q=q, k_win=k_win):
                start = SECOND - STEP * a
                mod = (q * k2[r, start : start + BLOCK, :]).astype(jnp.bfloat16)
                s = lax.dot_general(mod, k_win, (((1,), (1,)), ((), ())), preferred_element_type=jnp.float32)
                edge = jnp.where(upper, s[:, :HEAD], s[:, FIRST:])
                score[a % 2, r, :, :HEAD] = edge
                score[a % 2, r, :, HEAD:] = s[:, HEAD:FIRST]
                return jnp.maximum(
                    jnp.maximum(edge, s[:, HEAD : 2 * HEAD]),
                    jnp.maximum(s[:, 2 * HEAD : 3 * HEAD], s[:, 3 * HEAD : FIRST]),
                )

            def mixed(a, r, shift, v_win=v_win):
                start = SECOND - STEP * a
                parts = [
                    jnp.exp2(score[a % 2, r, :, k * HEAD : (k + 1) * HEAD] * SCALE - shift)
                    for k in range(FIRST // HEAD)
                ]
                nothing = jnp.zeros_like(parts[0])
                ends = [jnp.where(upper, parts[0], nothing), jnp.where(upper, nothing, parts[0])]
                weights = jnp.concatenate(ends[:1] + parts[1:] + ends[1:], axis=1).astype(jnp.bfloat16)
                mix = jnp.dot(weights, v_win, preferred_element_type=jnp.float32)
                return mix * v2[r, start : start + BLOCK, :]

            most = None
            for r in range(STEP):
                here = scored(0, r)
                most = here if most is None else jnp.maximum(most, here)
            for a in range(SECOND // STEP):
                new = jnp.max(most, axis=1, keepdims=True)
                if a > 0:
                    old = top[...]
                    new = jnp.maximum(old, new)
                else:
                    new = jnp.broadcast_to(new, (BLOCK, HEAD))
                top[...] = new
                shift = new * SCALE
                if a > 0:
                    shrink = jnp.exp2(old * SCALE - shift)
                    total[...] = total[...] * jnp.concatenate([shrink, shrink], axis=1)
                most = None
                for r in range(STEP):
                    if a + 1 < SECOND // STEP:
                        here = scored(a + 1, r)
                        most = here if most is None else jnp.maximum(most, here)
                    part = mixed(a, r, shift)
                    if a == 0 and r == 0:
                        total[...] = part
                    else:
                        total[...] += part
            out[base : base + BLOCK, g * HEAD : (g + 1) * HEAD] = (
                total[:, :HEAD] / total[:, HEAD:]
            ).astype(jnp.bfloat16)


def attention(index, *operands):
    vmem = pl.BlockSpec(memory_space=pltpu.VMEM)
    hbm = pl.BlockSpec(memory_space=pl.ANY)
    return pl.pallas_call(
        attend,
        out_shape=jax.ShapeDtypeStruct((ROWS, GROUP * HEAD), jnp.bfloat16),
        in_specs=[pl.BlockSpec(memory_space=pltpu.SMEM)] + [hbm] * 7,
        out_specs=vmem,
        scratch_shapes=[pltpu.VMEM(x.shape, x.dtype) for x in operands]
        + [
            pltpu.SemaphoreType.DMA((7,)),
            pltpu.VMEM((3 * ROWS, HEAD), jnp.bfloat16),
            pltpu.VMEM((3 * ROWS, 2 * HEAD), jnp.bfloat16),
            pltpu.VMEM((STEP, BLOCK + SECOND, HEAD), jnp.float32),
            pltpu.VMEM((STEP, BLOCK + SECOND, 2 * HEAD), jnp.float32),
            pltpu.VMEM((3, BLOCK + SECOND, HEAD), jnp.float32),
            pltpu.VMEM((2, STEP, BLOCK, FIRST), jnp.float32),
            pltpu.VMEM((BLOCK, 2 * HEAD), jnp.float32),
            pltpu.VMEM((BLOCK, HEAD), jnp.float32),
        ],
        cost_estimate=pl.CostEstimate(flops=12_000_000_000, bytes_accessed=1_000_000, transcendentals=9_000_000),
        name="attend",
    )(index, *operands)


def project(order, direct, swapped, weight, out, rows, held, total, sems):
    part = weight.shape[0] // CHUNKS
    copies = [
        pltpu.make_async_copy(weight.at[pl.ds(n * part, part)], held.at[pl.ds(n * part, part)], sems.at[n])
        for n in range(CHUNKS)
    ]
    for copy in copies:
        copy.start()
    for k in range(SIDE):
        at = order[k]
        rows[:, k * GROUP * HEAD : (k + 1) * GROUP * HEAD] = jnp.where(
            order[SIDE + k] == 0, direct[at], swapped[at]
        )
    for n in range(CHUNKS):
        copies[n].wait()
        to = slice(n * part, (n + 1) * part)
        piece = jnp.dot(rows[:, to], held[to, :], preferred_element_type=jnp.float32)
        if n == 0:
            total[...] = piece
        elif n < CHUNKS - 1:
            total[...] += piece
        else:
            out[...] = (total[...] + piece).astype(jnp.bfloat16)


def projection(order, direct, swapped, weight):
    depth, width = weight.shape
    vmem = pl.BlockSpec(memory_space=pltpu.VMEM)
    return pl.pallas_call(
        project,
        out_shape=jax.ShapeDtypeStruct((ROWS, width), jnp.bfloat16),
        in_specs=[pl.BlockSpec(memory_space=pltpu.SMEM)] + [vmem] * 2 + [pl.BlockSpec(memory_space=pl.ANY)],
        out_specs=vmem,
        scratch_shapes=[
            pltpu.VMEM((ROWS, depth), jnp.bfloat16),
            pltpu.VMEM((depth, width), jnp.bfloat16),
            pltpu.VMEM((ROWS, width), jnp.float32),
            pltpu.SemaphoreType.DMA((CHUNKS,)),
        ],
        compiler_params=pltpu.CompilerParams(vmem_limit_bytes=62 * 1024 * 1024),
        cost_estimate=pl.CostEstimate(flops=1_100_000_000, bytes_accessed=6_000_000, transcendentals=0),
        name="project",
    )(order, direct, swapped, weight)


CHUNKS = 2
SIDE = 8
CHIPS = 4
HOPS = (0, 1, 3, 2)
Z_GROUPS = [[y * SIDE + z for z in range(SIDE)] for y in range(SIDE)]
Y_GROUPS = [[y * SIDE + z for y in range(SIDE)] for z in range(SIDE)]


def spread(x, groups):
    copies = jnp.broadcast_to(x[None], (SIDE,) + x.shape)
    return lax.all_to_all(copies, "seq", split_axis=0, concat_axis=0, axis_index_groups=groups)


def shifted(x, by):
    size = lax.axis_size("seq")
    return lax.ppermute(x, "seq", [(i, i + by) for i in range(size - by)])


def pack(keys, values, second_keys, second_values, out, sems):
    tail = pl.ds(ROWS - SECOND, SECOND)
    moves = [
        pltpu.make_async_copy(keys, out.at[pl.ds(0, ROWS)], sems.at[0]),
        pltpu.make_async_copy(values, out.at[pl.ds(ROWS, ROWS)], sems.at[1]),
        pltpu.make_async_copy(second_keys.at[tail], out.at[pl.ds(2 * ROWS, SECOND)], sems.at[2]),
        pltpu.make_async_copy(second_values.at[tail], out.at[pl.ds(2 * ROWS + SECOND, SECOND)], sems.at[3]),
    ]
    for move in moves:
        move.start()
    for move in moves:
        move.wait()


def packing(*operands):
    return pl.pallas_call(
        pack,
        out_shape=jax.ShapeDtypeStruct((2 * ROWS + 2 * SECOND, HEAD), jnp.bfloat16),
        in_specs=[pl.BlockSpec(memory_space=pl.ANY)] * 4,
        out_specs=pl.BlockSpec(memory_space=pltpu.VMEM),
        scratch_shapes=[pltpu.SemaphoreType.DMA((4,))],
        cost_estimate=pl.CostEstimate(flops=0, bytes_accessed=300_000, transcendentals=0),
        name="pack",
    )(*operands)


def relay(block, out, sem):
    move = pltpu.make_async_copy(block, out, sem)
    move.start()
    move.wait()


def relayed(block):
    return pl.pallas_call(
        relay,
        out_shape=jax.ShapeDtypeStruct(block.shape, block.dtype),
        in_specs=[pl.BlockSpec(memory_space=pltpu.VMEM)],
        out_specs=pl.BlockSpec(memory_space=pl.ANY),
        scratch_shapes=[pltpu.SemaphoreType.DMA],
        compiler_params=pltpu.CompilerParams(vmem_limit_bytes=16 * 1024 * 1024),
        cost_estimate=pl.CostEstimate(flops=0, bytes_accessed=1_000_000, transcendentals=0),
        name="relay",
    )(block)


def on_device(queries, first_keys, first_values, second_keys, second_values, out_weight):
    width = out_weight.shape[1]
    packed = packing(first_keys, first_values, second_keys, second_values)
    near = shifted(packed, 1)
    far = shifted(packed, 2)
    block = spread(out_weight, Z_GROUPS)
    block = relayed(block)
    weight = lax.all_gather(
        block.reshape(ROWS, width), "seq", axis=0, tiled=True, axis_index_groups=Y_GROUPS
    )
    seq = lax.axis_index("seq").astype(jnp.int32)
    head = lax.axis_index("head").astype(jnp.int32)
    attended = attention(
        seq.reshape(1), queries, far, near, first_keys, first_values, second_keys, second_values
    )
    direct = [attended]
    for hop in HOPS[1:]:
        pairs = [(2 * x + c, 2 * ((x + hop) % CHIPS) + c) for x in range(CHIPS) for c in range(2)]
        direct.append(lax.ppermute(attended, "head", pairs))
    direct = jnp.stack(direct)
    swapped = lax.ppermute(direct, "head", [(2 * x + c, 2 * x + 1 - c) for x in range(CHIPS) for c in range(2)])
    chip, core = lax.div(head, 2), lax.rem(head, 2)
    owner = jnp.arange(SIDE, dtype=jnp.int32)
    distance = lax.rem(chip - lax.div(owner, 2) + CHIPS, CHIPS)
    place = jnp.where(distance < 2, distance, 5 - distance)
    part = jnp.where(lax.rem(owner, 2) == core, 0, 1)
    order = jnp.concatenate([place, part]).astype(jnp.int32)
    return attended, projection(order, direct, swapped, weight)


def solution(mesh):
    spec = P("seq", "head")

    return jax.shard_map(on_device, mesh=mesh, in_specs=(spec,) * 6, out_specs=(spec, spec), check_vma=False)
```

time: 115 us -> 110 us (0.957)
  the two profiles are of different devices: /device:TPU:2 before, /device:TPU:33 now
where the time goes in v2:
time: 110 us
  Pallas kernels  28 us (25%)
  blocking collectives  25.9 us (24%)
  starting transfers between devices  21.9 us (20%)
  waiting for transfers between devices  15.5 us (14%)
  between operations  14.2 us (13%)
  local copies, waits for them, and re-layouts  2.35 us (2%)
  other arithmetic  1.59 us (1%)
    all_to_all x1, blocking collectives, spread(): lax.all_to_all(copies, 'seq', split_axis=0, concat_axis=0, axis_index_gro...  25.9 us
    pallas_call x1, Pallas kernels, attention(): pl.pallas_call(attend, out_shape=jax.ShapeDtypeStruct((ROWS, GROUP * HEAD...  20.7 us
    ppermute x3, starting transfers between devices, on_device(): direct.append(lax.ppermute(attended, 'head', pairs))  9.94 us
    ppermute x2, waiting for transfers between devices, shifted(): return lax.ppermute(x, 'seq', [(i, i + by) for i in range(size - by)])  9.59 us
    ppermute x1, starting transfers between devices, on_device(): lax.ppermute(direct, 'head', [(2 * x + c, 2 * x + 1 - c) for x in range(C...  7.34 us
    ppermute x3, waiting for transfers between devices, on_device(): direct.append(lax.ppermute(attended, 'head', pairs))  5 us
    pallas_call x1, Pallas kernels, projection(): pl.pallas_call(project, out_shape=jax.ShapeDtypeStruct((ROWS, width), jnp...  4.95 us
    ppermute x2, starting transfers between devices, shifted(): return lax.ppermute(x, 'seq', [(i, i + by) for i in range(size - by)])  4.63 us
  transfers between devices with their start and end apart: 7, of which 5 were waited for; matrix products, arithmetic and copies ran while one was open for 1% of the time, Pallas kernels for 20%

profile of v2, /device:TPU:33, one launch (start us, length us, event | category | flops | bytes accessed | tf_op | source)
XLA Modules:
  0.0 109.5 jit_solution(10046531407164010473)
XLA Ops:
  7.2 0.0 all-gather.2.cloned.1.call-start
  7.2 0.9 broadcast_in_dim.4
  8.1 25.9 %all_to_all.5.block = bf16[8,32,1024]{2,1,0:T(8,128)(2,1)S(1)} all-to-all(bf16[8,32,1024]{2,1,0:T(8,128)(2,1)S(1)} %broadcast_in_dim.4), channel_id=1, replica_groups={{0,8,16,24,32,40,48,56},{64,72,80,88,96,104,112,120},{128,136,144,152,1..., dimensions={0} | all-to-all | bytes 1048576 | tf_op jit(solution)/shard_map/all_to_all | solution.py:213
  34.1 0.8 relay.1
  34.9 0.0 all-gather.2.cloned.1.call-update
  34.9 1.6 %pack.1 = bf16[576,128]{1,0:T(8,128)(2,1)} custom-call(bf16[256,128]{1,0:T(8,128)(2,1)} %refs_3_.1, bf16[256,128]{1,0:T(8,128)(2,1)} %refs_4_.1, bf16[256,128]{1,0:T(8,128)(2,1)} %refs_5_.1, bf16[256,128]{1,0:T(8,128)(2,1)} %refs_6_.1), custom_call_target="tpu_custom_call" | custom-call | bytes 300000 | tf_op jit(solution)/shard_map/pack/pallas_call | solution.py:236
  36.5 1.9 %collective-permute-start.1 = (bf16[576,128]{1,0:T(8,128)(2,1)}, bf16[576,128]{1,0:T(8,128)(2,1)S(1)}, u32[]{:S(2)}, u32[]{:S(2)}) collective-permute-start(bf16[576,128]{1,0:T(8,128)(2,1)} %pack.1), channel_id=1, source_target_pairs={{0,8},{8,16},{16,24},{24,32},{32,40},{40,48},{48,56},{56,64},{64,7... | collective-permute-start | bytes 442376 | tf_op jit(solution)/shard_map/ppermute | solution.py:218
  38.4 2.7 %collective-permute-start = (bf16[576,128]{1,0:T(8,128)(2,1)}, bf16[576,128]{1,0:T(8,128)(2,1)S(1)}, u32[]{:S(2)}, u32[]{:S(2)}) collective-permute-start(bf16[576,128]{1,0:T(8,128)(2,1)} %pack.1), channel_id=1, source_target_pairs={{0,16},{8,24},{16,32},{24,40},{32,48},{40,56},{48,64},{56,72},{64,... | collective-permute-start | bytes 442376 | tf_op jit(solution)/shard_map/ppermute | solution.py:218
  41.1 4.8 %collective-permute-done.1.refs_2_ = bf16[576,128]{1,0:T(8,128)(2,1)S(1)} collective-permute-done((bf16[576,128]{1,0:T(8,128)(2,1)}, bf16[576,128]{1,0:T(8,128)(2,1)S(1)}, u32[]{:S(2)}, u32[]{:S(2)}) %collective-permute-start.1) | collective-permute-done | bytes 147488 | tf_op jit(solution)/shard_map/ppermute | solution.py:218
  45.9 0.0 copy-start.2
  45.9 4.8 %collective-permute-done.refs_1_ = bf16[576,128]{1,0:T(8,128)(2,1)S(1)} collective-permute-done((bf16[576,128]{1,0:T(8,128)(2,1)}, bf16[576,128]{1,0:T(8,128)(2,1)S(1)}, u32[]{:S(2)}, u32[]{:S(2)}) %collective-permute-start) | collective-permute-done | bytes 147488 | tf_op jit(solution)/shard_map/ppermute | solution.py:218
  50.7 0.0 copy-start.3
  50.7 0.0 copy-done.2
  50.7 0.7 copy-done.3
  51.4 20.7 %attend.1 = bf16[256,256]{1,0:T(8,128)(2,1)} custom-call(s32[1]{0:T(128)} %bitcast.index, bf16[256,256]{1,0:T(8,128)(2,1)} %refs_0_.1, bf16[576,128]{1,0:T(8,128)(2,1)} %copy-done.3, bf16[576,128]{1,0:T(8,128)(2,1)} %copy-done.2, bf16[256,128]{1,0:T(8,128)(2,1)} %refs_3_.1, bf16[256,128]{1,0:T(8,128)(2,1)} %refs_4_.1, bf16[256,128]{1,0:T(8,128)(2,1)} %refs_5_.1, ...), custom_call_target="tpu_custom_call" | custom-call | flops 12000000000 | bytes 1000000 | tf_op jit(solution)/shard_map/attend/pallas_call | solution.py:136
  72.1 4.7 %collective-permute-start.4 = (bf16[256,256]{1,0:T(8,128)(2,1)}, bf16[256,256]{1,0:T(8,128)(2,1)S(1)}, u32[]{:S(2)}, u32[]{:S(2)}) collective-permute-start(bf16[256,256]{1,0:T(8,128)(2,1)} %attend.1), channel_id=1, source_target_pairs={{0,4},{1,5},{2,6},{3,7},{4,0},{5,1},{6,2},{7,3},{8,12},{9,13},{10,... | collective-permute-start | bytes 393224 | tf_op jit(solution)/shard_map/ppermute | solution.py:284
  76.8 2.8 %collective-permute-start.3 = (bf16[256,256]{1,0:T(8,128)(2,1)}, bf16[256,256]{1,0:T(8,128)(2,1)S(1)}, u32[]{:S(2)}, u32[]{:S(2)}) collective-permute-start(bf16[256,256]{1,0:T(8,128)(2,1)} %attend.1), channel_id=1, source_target_pairs={{0,6},{1,7},{2,0},{3,1},{4,2},{5,3},{6,4},{7,5},{8,14},{9,15},{10,... | collective-permute-start | bytes 393224 | tf_op jit(solution)/shard_map/ppermute | solution.py:284
  79.5 2.5 %collective-permute-start.2 = (bf16[256,256]{1,0:T(8,128)(2,1)}, bf16[256,256]{1,0:T(8,128)(2,1)S(1)}, u32[]{:S(2)}, u32[]{:S(2)}) collective-permute-start(bf16[256,256]{1,0:T(8,128)(2,1)} %attend.1), channel_id=1, source_target_pairs={{0,2},{1,3},{2,4},{3,5},{4,6},{5,7},{6,0},{7,1},{8,10},{9,11},{10,... | collective-permute-start | bytes 393224 | tf_op jit(solution)/shard_map/ppermute | solution.py:284
  82.0 0.0 collective-permute-done.4
  82.1 1.0 collective-permute-done.3
  83.1 4.0 %collective-permute-done.2 = bf16[256,256]{1,0:T(8,128)(2,1)S(1)} collective-permute-done((bf16[256,256]{1,0:T(8,128)(2,1)}, bf16[256,256]{1,0:T(8,128)(2,1)S(1)}, u32[]{:S(2)}, u32[]{:S(2)}) %collective-permute-start.2) | collective-permute-done | bytes 131104 | tf_op jit(solution)/shard_map/ppermute | solution.py:284
  87.1 1.0 pad_maximum_fusion.direct
  88.0 0.0 copy-start
  88.0 7.3 %collective-permute-start.5 = (bf16[4,256,256]{2,1,0:T(8,128)(2,1)S(1)}, bf16[4,256,256]{2,1,0:T(8,128)(2,1)S(1)}, u32[]{:S(2)}, u32[]{:S(2)}) collective-permute-start(bf16[4,256,256]{2,1,0:T(8,128)(2,1)S(1)} %pad_maximum_fusion.direct), channel_id=1, source_target_pairs={{0,1},{1,0},{2,3},{3,2},{4,5},{5,4},{6,7},{7,6},{8,9},{9,8},{10,11... | collective-permute-start | bytes 1572872 | tf_op jit(solution)/shard_map/ppermute | solution.py:286
  95.4 0.6 pad_add_fusion.order
  96.0 0.9 collective-permute-done.5.swapped
  96.9 0.0 copy-start.1
  96.9 0.0 all-gather.2.cloned.1.call-done.weight
  96.9 0.0 copy-done
  96.9 0.8 copy-done.1
  97.7 4.9 %project.1 = bf16[256,1024]{1,0:T(8,128)(2,1)} custom-call(s32[16]{0:T(128)} %pad_add_fusion.order, bf16[4,256,256]{2,1,0:T(8,128)(2,1)} %copy-done, bf16[4,256,256]{2,1,0:T(8,128)(2,1)} %copy-done.1, bf16[2048,1024]{1,0:T(8,128)(2,1)} %all-gather.2.cloned.1.call-done.weight), custom_call_target="tpu_custom_call" | custom-call | flops 1100000000 | bytes 6000000 | tf_op jit(solution)/shard_map/project/pallas_call | solution.py:186
  (1 shorter events, 0.0 us)
Async XLA Ops:
  7.2 89.7 %all-gather.2.cloned.1.call-start = ((), (), s32[]{:S(2)}) async-start(), calls=%async_computation.1 | async-start | bytes 4718592 | tf_op jit(solution)/shard_map/all_gather | solution.py:273
  36.5 9.4 %collective-permute-start.1 = (bf16[576,128]{1,0:T(8,128)(2,1)}, bf16[576,128]{1,0:T(8,128)(2,1)S(1)}, u32[]{:S(2)}, u32[]{:S(2)}) collective-permute-start(bf16[576,128]{1,0:T(8,128)(2,1)} %pack.1), channel_id=1, source_target_pairs={{0,8},{8,16},{16,24},{24,32},{32,40},{40,48},{48,56},{56,64},{64,7... | collective-permute-start | bytes 442376 | tf_op jit(solution)/shard_map/ppermute | solution.py:218
  38.4 12.3 %collective-permute-start = (bf16[576,128]{1,0:T(8,128)(2,1)}, bf16[576,128]{1,0:T(8,128)(2,1)S(1)}, u32[]{:S(2)}, u32[]{:S(2)}) collective-permute-start(bf16[576,128]{1,0:T(8,128)(2,1)} %pack.1), channel_id=1, source_target_pairs={{0,16},{8,24},{16,32},{24,40},{32,48},{40,56},{48,64},{56,72},{64,... | collective-permute-start | bytes 442376 | tf_op jit(solution)/shard_map/ppermute | solution.py:218
  45.9 4.8 %copy-start.2 = (bf16[576,128]{1,0:T(8,128)(2,1)}, bf16[576,128]{1,0:T(8,128)(2,1)S(1)}, u32[]{:S(2)}) copy-start(bf16[576,128]{1,0:T(8,128)(2,1)S(1)} %collective-permute-done.1.refs_2_) | copy-start | bytes 442372
  50.7 0.7 copy-start.3
  72.1 10.0 %collective-permute-start.4 = (bf16[256,256]{1,0:T(8,128)(2,1)}, bf16[256,256]{1,0:T(8,128)(2,1)S(1)}, u32[]{:S(2)}, u32[]{:S(2)}) collective-permute-start(bf16[256,256]{1,0:T(8,128)(2,1)} %attend.1), channel_id=1, source_target_pairs={{0,4},{1,5},{2,6},{3,7},{4,0},{5,1},{6,2},{7,3},{8,12},{9,13},{10,... | collective-permute-start | bytes 393224 | tf_op jit(solution)/shard_map/ppermute | solution.py:284
  76.8 6.3 %collective-permute-start.3 = (bf16[256,256]{1,0:T(8,128)(2,1)}, bf16[256,256]{1,0:T(8,128)(2,1)S(1)}, u32[]{:S(2)}, u32[]{:S(2)}) collective-permute-start(bf16[256,256]{1,0:T(8,128)(2,1)} %attend.1), channel_id=1, source_target_pairs={{0,6},{1,7},{2,0},{3,1},{4,2},{5,3},{6,4},{7,5},{8,14},{9,15},{10,... | collective-permute-start | bytes 393224 | tf_op jit(solution)/shard_map/ppermute | solution.py:284
  79.5 7.5 %collective-permute-start.2 = (bf16[256,256]{1,0:T(8,128)(2,1)}, bf16[256,256]{1,0:T(8,128)(2,1)S(1)}, u32[]{:S(2)}, u32[]{:S(2)}) collective-permute-start(bf16[256,256]{1,0:T(8,128)(2,1)} %attend.1), channel_id=1, source_target_pairs={{0,2},{1,3},{2,4},{3,5},{4,6},{5,7},{6,0},{7,1},{8,10},{9,11},{10,... | collective-permute-start | bytes 393224 | tf_op jit(solution)/shard_map/ppermute | solution.py:284
  88.0 8.9 %copy-start = (bf16[4,256,256]{2,1,0:T(8,128)(2,1)}, bf16[4,256,256]{2,1,0:T(8,128)(2,1)S(1)}, u32[]{:S(2)}) copy-start(bf16[4,256,256]{2,1,0:T(8,128)(2,1)S(1)} %pad_maximum_fusion.direct) | copy-start | bytes 1572868
  88.0 8.9 %collective-permute-start.5 = (bf16[4,256,256]{2,1,0:T(8,128)(2,1)S(1)}, bf16[4,256,256]{2,1,0:T(8,128)(2,1)S(1)}, u32[]{:S(2)}, u32[]{:S(2)}) collective-permute-start(bf16[4,256,256]{2,1,0:T(8,128)(2,1)S(1)} %pad_maximum_fusion.direct), channel_id=1, source_target_pairs={{0,1},{1,0},{2,3},{3,2},{4,5},{5,4},{6,7},{7,6},{8,9},{9,8},{10,11... | collective-permute-start | bytes 1572872 | tf_op jit(solution)/shard_map/ppermute | solution.py:286
  96.9 0.8 copy-start.1
Sparse Core Ops, SparseCore 0:
  35.0 52.0 all-gather.1

commit v3 on v2

--- a/solution.py
+++ b/solution.py
@@ -208,8 +208,22 @@
 Y_GROUPS = [[y * SIDE + z for y in range(SIDE)] for z in range(SIDE)]
 
 
+def repeat(x, out):
+    for k in range(SIDE):
+        out[k] = x[...]
+
+
 def spread(x, groups):
-    copies = jnp.broadcast_to(x[None], (SIDE,) + x.shape)
+    vmem = pl.BlockSpec(memory_space=pltpu.VMEM)
+    copies = pl.pallas_call(
+        repeat,
+        out_shape=jax.ShapeDtypeStruct((SIDE,) + x.shape, x.dtype),
+        in_specs=[vmem],
+        out_specs=vmem,
+        compiler_params=pltpu.CompilerParams(vmem_limit_bytes=16 * 1024 * 1024),
+        cost_estimate=pl.CostEstimate(flops=0, bytes_accessed=600_000, transcendentals=0),
+        name="repeat",
+    )(x)
     return lax.all_to_all(copies, "seq", split_axis=0, concat_axis=0, axis_index_groups=groups)
 
 

time: 110 us -> 110 us (level)
    unnamed x8 -> x10, local copies, waits for them, and re-layouts: 1.46 us -> 2.29 us
where the time goes in v3:
time: 110 us; the launch traced here: 109 us
  Pallas kernels  28 us (25%)
  blocking collectives  25.9 us (24%)
  starting transfers between devices  21.9 us (20%)
  waiting for transfers between devices  15.5 us (14%)
  between operations  14.2 us (13%)
  local copies, waits for them, and re-layouts  2.29 us (2%)
  other arithmetic  1.59 us (1%)
    all_to_all x1, blocking collectives, spread(): lax.all_to_all(copies, 'seq', split_axis=0, concat_axis=0, axis_index_gro...  25.9 us
    pallas_call x1, Pallas kernels, attention(): pl.pallas_call(attend, out_shape=jax.ShapeDtypeStruct((ROWS, GROUP * HEAD...  20.7 us
    ppermute x3, starting transfers between devices, on_device(): direct.append(lax.ppermute(attended, 'head', pairs))  9.94 us
    ppermute x2, waiting for transfers between devices, shifted(): return lax.ppermute(x, 'seq', [(i, i + by) for i in range(size - by)])  9.59 us
    ppermute x1, starting transfers between devices, on_device(): lax.ppermute(direct, 'head', [(2 * x + c, 2 * x + 1 - c) for x in range(C...  7.31 us
    ppermute x3, waiting for transfers between devices, on_device(): direct.append(lax.ppermute(attended, 'head', pairs))  5.01 us
    pallas_call x1, Pallas kernels, projection(): pl.pallas_call(project, out_shape=jax.ShapeDtypeStruct((ROWS, width), jnp...  4.95 us
    ppermute x2, starting transfers between devices, shifted(): return lax.ppermute(x, 'seq', [(i, i + by) for i in range(size - by)])  4.63 us
  transfers between devices with their start and end apart: 7, of which 5 were waited for; matrix products, arithmetic and copies ran while one was open for 1% of the time, Pallas kernels for 20%

profile of v3, /device:TPU:33, one launch (start us, length us, event | category | flops | bytes accessed | tf_op | source)
XLA Modules:
  0.0 109.5 jit_solution(8962489940055004238)
XLA Ops:
  7.2 0.0 all-gather.2.cloned.1.call-start
  7.2 0.0 copy-start
  7.2 0.8 copy-done
  8.1 25.9 %all_to_all.5.block = bf16[8,32,1024]{2,1,0:T(8,128)(2,1)S(1)} all-to-all(bf16[8,32,1024]{2,1,0:T(8,128)(2,1)S(1)} %repeat.1), channel_id=1, replica_groups={{0,8,16,24,32,40,48,56},{64,72,80,88,96,104,112,120},{128,136,144,152,1..., dimensions={0} | all-to-all | bytes 1048576 | tf_op jit(solution)/shard_map/all_to_all | solution.py:227
  34.0 0.8 relay.1
  34.8 0.0 all-gather.2.cloned.1.call-update
  34.9 1.6 %pack.1 = bf16[576,128]{1,0:T(8,128)(2,1)} custom-call(bf16[256,128]{1,0:T(8,128)(2,1)} %refs_3_.1, bf16[256,128]{1,0:T(8,128)(2,1)} %refs_4_.1, bf16[256,128]{1,0:T(8,128)(2,1)} %refs_5_.1, bf16[256,128]{1,0:T(8,128)(2,1)} %refs_6_.1), custom_call_target="tpu_custom_call" | custom-call | bytes 300000 | tf_op jit(solution)/shard_map/pack/pallas_call | solution.py:250
  36.4 1.9 %collective-permute-start.1 = (bf16[576,128]{1,0:T(8,128)(2,1)}, bf16[576,128]{1,0:T(8,128)(2,1)S(1)}, u32[]{:S(2)}, u32[]{:S(2)}) collective-permute-start(bf16[576,128]{1,0:T(8,128)(2,1)} %pack.1), channel_id=1, source_target_pairs={{0,8},{8,16},{16,24},{24,32},{32,40},{40,48},{48,56},{56,64},{64,7... | collective-permute-start | bytes 442376 | tf_op jit(solution)/shard_map/ppermute | solution.py:232
  38.4 2.7 %collective-permute-start = (bf16[576,128]{1,0:T(8,128)(2,1)}, bf16[576,128]{1,0:T(8,128)(2,1)S(1)}, u32[]{:S(2)}, u32[]{:S(2)}) collective-permute-start(bf16[576,128]{1,0:T(8,128)(2,1)} %pack.1), channel_id=1, source_target_pairs={{0,16},{8,24},{16,32},{24,40},{32,48},{40,56},{48,64},{56,72},{64,... | collective-permute-start | bytes 442376 | tf_op jit(solution)/shard_map/ppermute | solution.py:232
  41.1 4.8 %collective-permute-done.1.refs_2_ = bf16[576,128]{1,0:T(8,128)(2,1)S(1)} collective-permute-done((bf16[576,128]{1,0:T(8,128)(2,1)}, bf16[576,128]{1,0:T(8,128)(2,1)S(1)}, u32[]{:S(2)}, u32[]{:S(2)}) %collective-permute-start.1) | collective-permute-done | bytes 147488 | tf_op jit(solution)/shard_map/ppermute | solution.py:232
  45.9 0.0 copy-start.3
  45.9 4.8 %collective-permute-done.refs_1_ = bf16[576,128]{1,0:T(8,128)(2,1)S(1)} collective-permute-done((bf16[576,128]{1,0:T(8,128)(2,1)}, bf16[576,128]{1,0:T(8,128)(2,1)S(1)}, u32[]{:S(2)}, u32[]{:S(2)}) %collective-permute-start) | collective-permute-done | bytes 147488 | tf_op jit(solution)/shard_map/ppermute | solution.py:232
  50.7 0.0 copy-start.4
  50.7 0.0 copy-done.3
  50.7 0.7 copy-done.4
  51.4 20.7 %attend.1 = bf16[256,256]{1,0:T(8,128)(2,1)} custom-call(s32[1]{0:T(128)} %bitcast.index, bf16[256,256]{1,0:T(8,128)(2,1)} %refs_0_.1, bf16[576,128]{1,0:T(8,128)(2,1)} %copy-done.4, bf16[576,128]{1,0:T(8,128)(2,1)} %copy-done.3, bf16[256,128]{1,0:T(8,128)(2,1)} %refs_3_.1, bf16[256,128]{1,0:T(8,128)(2,1)} %refs_4_.1, bf16[256,128]{1,0:T(8,128)(2,1)} %refs_5_.1, ...), custom_call_target="tpu_custom_call" | custom-call | flops 12000000000 | bytes 1000000 | tf_op jit(solution)/shard_map/attend/pallas_call | solution.py:136
  72.0 4.7 %collective-permute-start.4 = (bf16[256,256]{1,0:T(8,128)(2,1)}, bf16[256,256]{1,0:T(8,128)(2,1)S(1)}, u32[]{:S(2)}, u32[]{:S(2)}) collective-permute-start(bf16[256,256]{1,0:T(8,128)(2,1)} %attend.1), channel_id=1, source_target_pairs={{0,4},{1,5},{2,6},{3,7},{4,0},{5,1},{6,2},{7,3},{8,12},{9,13},{10,... | collective-permute-start | bytes 393224 | tf_op jit(solution)/shard_map/ppermute | solution.py:298
  76.7 2.8 %collective-permute-start.3 = (bf16[256,256]{1,0:T(8,128)(2,1)}, bf16[256,256]{1,0:T(8,128)(2,1)S(1)}, u32[]{:S(2)}, u32[]{:S(2)}) collective-permute-start(bf16[256,256]{1,0:T(8,128)(2,1)} %attend.1), channel_id=1, source_target_pairs={{0,6},{1,7},{2,0},{3,1},{4,2},{5,3},{6,4},{7,5},{8,14},{9,15},{10,... | collective-permute-start | bytes 393224 | tf_op jit(solution)/shard_map/ppermute | solution.py:298
  79.5 2.5 %collective-permute-start.2 = (bf16[256,256]{1,0:T(8,128)(2,1)}, bf16[256,256]{1,0:T(8,128)(2,1)S(1)}, u32[]{:S(2)}, u32[]{:S(2)}) collective-permute-start(bf16[256,256]{1,0:T(8,128)(2,1)} %attend.1), channel_id=1, source_target_pairs={{0,2},{1,3},{2,4},{3,5},{4,6},{5,7},{6,0},{7,1},{8,10},{9,11},{10,... | collective-permute-start | bytes 393224 | tf_op jit(solution)/shard_map/ppermute | solution.py:298
  82.0 0.0 collective-permute-done.4
  82.0 1.0 collective-permute-done.3
  83.0 4.0 %collective-permute-done.2 = bf16[256,256]{1,0:T(8,128)(2,1)S(1)} collective-permute-done((bf16[256,256]{1,0:T(8,128)(2,1)}, bf16[256,256]{1,0:T(8,128)(2,1)S(1)}, u32[]{:S(2)}, u32[]{:S(2)}) %collective-permute-start.2) | collective-permute-done | bytes 131104 | tf_op jit(solution)/shard_map/ppermute | solution.py:298
  87.0 1.0 pad_maximum_fusion.direct
  88.0 0.0 copy-start.1
  88.0 7.3 %collective-permute-start.5 = (bf16[4,256,256]{2,1,0:T(8,128)(2,1)S(1)}, bf16[4,256,256]{2,1,0:T(8,128)(2,1)S(1)}, u32[]{:S(2)}, u32[]{:S(2)}) collective-permute-start(bf16[4,256,256]{2,1,0:T(8,128)(2,1)S(1)} %pad_maximum_fusion.direct), channel_id=1, source_target_pairs={{0,1},{1,0},{2,3},{3,2},{4,5},{5,4},{6,7},{7,6},{8,9},{9,8},{10,11... | collective-permute-start | bytes 1572872 | tf_op jit(solution)/shard_map/ppermute | solution.py:300
  95.4 0.6 pad_add_fusion.order
  96.0 0.9 collective-permute-done.5.swapped
  96.8 0.0 copy-start.2
  96.8 0.0 all-gather.2.cloned.1.call-done.weight
  96.9 0.0 copy-done.1
  96.9 0.8 copy-done.2
  97.6 5.0 %project.1 = bf16[256,1024]{1,0:T(8,128)(2,1)} custom-call(s32[16]{0:T(128)} %pad_add_fusion.order, bf16[4,256,256]{2,1,0:T(8,128)(2,1)} %copy-done.1, bf16[4,256,256]{2,1,0:T(8,128)(2,1)} %copy-done.2, bf16[2048,1024]{1,0:T(8,128)(2,1)} %all-gather.2.cloned.1.call-done.weight), custom_call_target="tpu_custom_call" | custom-call | flops 1100000000 | bytes 6000000 | tf_op jit(solution)/shard_map/project/pallas_call | solution.py:186
  (2 shorter events, 0.0 us)
Async XLA Ops:
  7.2 89.7 %all-gather.2.cloned.1.call-start = ((), (), s32[]{:S(2)}) async-start(), calls=%async_computation.1 | async-start | bytes 4718592 | tf_op jit(solution)/shard_map/all_gather | solution.py:287
  7.2 0.8 copy-start
  36.4 9.4 %collective-permute-start.1 = (bf16[576,128]{1,0:T(8,128)(2,1)}, bf16[576,128]{1,0:T(8,128)(2,1)S(1)}, u32[]{:S(2)}, u32[]{:S(2)}) collective-permute-start(bf16[576,128]{1,0:T(8,128)(2,1)} %pack.1), channel_id=1, source_target_pairs={{0,8},{8,16},{16,24},{24,32},{32,40},{40,48},{48,56},{56,64},{64,7... | collective-permute-start | bytes 442376 | tf_op jit(solution)/shard_map/ppermute | solution.py:232
  38.4 12.3 %collective-permute-start = (bf16[576,128]{1,0:T(8,128)(2,1)}, bf16[576,128]{1,0:T(8,128)(2,1)S(1)}, u32[]{:S(2)}, u32[]{:S(2)}) collective-permute-start(bf16[576,128]{1,0:T(8,128)(2,1)} %pack.1), channel_id=1, source_target_pairs={{0,16},{8,24},{16,32},{24,40},{32,48},{40,56},{48,64},{56,72},{64,... | collective-permute-start | bytes 442376 | tf_op jit(solution)/shard_map/ppermute | solution.py:232
  45.9 4.8 %copy-start.3 = (bf16[576,128]{1,0:T(8,128)(2,1)}, bf16[576,128]{1,0:T(8,128)(2,1)S(1)}, u32[]{:S(2)}) copy-start(bf16[576,128]{1,0:T(8,128)(2,1)S(1)} %collective-permute-done.1.refs_2_) | copy-start | bytes 442372
  50.7 0.7 copy-start.4
  72.0 10.0 %collective-permute-start.4 = (bf16[256,256]{1,0:T(8,128)(2,1)}, bf16[256,256]{1,0:T(8,128)(2,1)S(1)}, u32[]{:S(2)}, u32[]{:S(2)}) collective-permute-start(bf16[256,256]{1,0:T(8,128)(2,1)} %attend.1), channel_id=1, source_target_pairs={{0,4},{1,5},{2,6},{3,7},{4,0},{5,1},{6,2},{7,3},{8,12},{9,13},{10,... | collective-permute-start | bytes 393224 | tf_op jit(solution)/shard_map/ppermute | solution.py:298
  76.7 6.3 %collective-permute-start.3 = (bf16[256,256]{1,0:T(8,128)(2,1)}, bf16[256,256]{1,0:T(8,128)(2,1)S(1)}, u32[]{:S(2)}, u32[]{:S(2)}) collective-permute-start(bf16[256,256]{1,0:T(8,128)(2,1)} %attend.1), channel_id=1, source_target_pairs={{0,6},{1,7},{2,0},{3,1},{4,2},{5,3},{6,4},{7,5},{8,14},{9,15},{10,... | collective-permute-start | bytes 393224 | tf_op jit(solution)/shard_map/ppermute | solution.py:298
  79.5 7.5 %collective-permute-start.2 = (bf16[256,256]{1,0:T(8,128)(2,1)}, bf16[256,256]{1,0:T(8,128)(2,1)S(1)}, u32[]{:S(2)}, u32[]{:S(2)}) collective-permute-start(bf16[256,256]{1,0:T(8,128)(2,1)} %attend.1), channel_id=1, source_target_pairs={{0,2},{1,3},{2,4},{3,5},{4,6},{5,7},{6,0},{7,1},{8,10},{9,11},{10,... | collective-permute-start | bytes 393224 | tf_op jit(solution)/shard_map/ppermute | solution.py:298
  88.0 8.8 %copy-start.1 = (bf16[4,256,256]{2,1,0:T(8,128)(2,1)}, bf16[4,256,256]{2,1,0:T(8,128)(2,1)S(1)}, u32[]{:S(2)}) copy-start(bf16[4,256,256]{2,1,0:T(8,128)(2,1)S(1)} %pad_maximum_fusion.direct) | copy-start | bytes 1572868
  88.0 8.8 %collective-permute-start.5 = (bf16[4,256,256]{2,1,0:T(8,128)(2,1)S(1)}, bf16[4,256,256]{2,1,0:T(8,128)(2,1)S(1)}, u32[]{:S(2)}, u32[]{:S(2)}) collective-permute-start(bf16[4,256,256]{2,1,0:T(8,128)(2,1)S(1)} %pad_maximum_fusion.direct), channel_id=1, source_target_pairs={{0,1},{1,0},{2,3},{3,2},{4,5},{5,4},{6,7},{7,6},{8,9},{9,8},{10,11... | collective-permute-start | bytes 1572872 | tf_op jit(solution)/shard_map/ppermute | solution.py:300
  96.8 0.8 copy-start.2
Sparse Core Ops, SparseCore 0:
  35.0 52.0 all-gather.1
